TPU v7x, 512 devices: a whole 4x4x16 slice. The times are simulated.
512 devices in a mesh: freq: 32 (over z_lo, x), src: 2 (over z_hi), rcv: 8 (over y, core).
Axes of the slice: x: 4, y: 4, z: 16 (z_hi: 2, z_lo: 8; z = z_hi * 8 + z_lo), core: 2. Of those that a mesh axis runs over, the one named last changes fastest.
Arguments:
- traces: float32 [1024, 1024, 256], P(('src', 'freq'), 'rcv'), may hold values from -6 to 6
Outputs:
- multiples: float32 [2, 96, 1024, 1024], P(None, 'freq', 'src', 'rcv')
All inputs are finite; a program needn't handle non-finite values.
Results may differ from a plain program's by a relative error of at most 0.000098.
Values sent between devices are 32-bit elements; how exact they have to be, the bound alone decides.
A program may use at most 64 MiB of HBM per device.

v0:
```python
import math
import jax
import jax.numpy as jnp
from jax import lax
from jax.sharding import PartitionSpec as P

N = 1024
FPD = 3


def dft_matrix(n_time, n_freq):
    times = jnp.arange(n_time, dtype=jnp.int32)
    bins = jnp.arange(n_freq, dtype=jnp.int32)
    phase = times[:, None] * bins[None, :] % n_time
    angle = phase.astype(jnp.float32) * (2.0 * math.pi / n_time)
    both = jnp.stack([jnp.cos(angle), -jnp.sin(angle)], axis=-1)
    return both.reshape(n_time, 2 * n_freq) * (1.0 / math.sqrt(n_time))


def batched_dot(left, right):
    return jnp.einsum(
        "mgq,mqn->mgn",
        left,
        right,
        precision=lax.Precision.HIGHEST,
        preferred_element_type=jnp.float32,
    )


def complex_product(left_re, left_im, right_re, right_im):
    real_part = batched_dot(left_re, right_re) - batched_dot(left_im, right_im)
    imag_part = batched_dot(left_re, right_im) + batched_dot(left_im, right_re)
    return (real_part, imag_part)


def per_device(traces):
    n_time = traces.shape[2]
    n_freq = FPD * lax.axis_size("freq")
    dft_table = dft_matrix(n_time, n_freq)
    spectra = jnp.einsum(
        "srt,tk->ksr",
        traces,
        dft_table,
        precision=lax.Precision.HIGHEST,
        preferred_element_type=jnp.float32,
    )
    regrouped = lax.all_to_all(spectra, "freq", split_axis=0, concat_axis=1, tiled=True)
    src_rows = regrouped.shape[1]
    rcv_cols = regrouped.shape[2]
    split_parts = regrouped.reshape(FPD, 2, src_rows, rcv_cols)
    local_re = split_parts[:, 0]
    local_im = split_parts[:, 1]
    col_re, col_im = (
        lax.all_gather(local_re, "src", axis=1, tiled=True),
        lax.all_gather(local_im, "src", axis=1, tiled=True),
    )
    piece_re = lax.all_gather(local_re, "rcv", axis=2, tiled=True)
    piece_im = lax.all_gather(local_im, "rcv", axis=2, tiled=True)
    real_part, imag_part = complex_product(piece_re, piece_im, col_re, col_im)
    scale = -1.0 / math.sqrt(N)
    return jnp.stack([real_part, imag_part]) * scale


def solution(mesh):
    in_specs = (P(("src", "freq"), "rcv", None),)
    out_specs = P(None, "freq", "src", "rcv")
    return jax.shard_map(
        per_device, mesh=mesh, in_specs=in_specs, out_specs=out_specs, check_vma=False
    )
```

profile of v0, /device:TPU:1, one launch (start us, length us, event | category | flops | bytes accessed | tf_op | source)
XLA Modules:
  0.0 411.7 jit_solution(3908307167513742405)
XLA Ops:
  6.5 0.0 copy-start
  6.5 0.0 all-gather.11.cloned.1.call-start
  6.5 0.4 sine_negate_fusion
  7.0 0.2 copy.14
  7.1 0.1 reshape.83
  7.3 0.8 copy-done
  8.1 2.3 fusion.39
  10.4 0.9 copy.15
  11.3 89.4 %all_to_all.15 = f32[192,16,128]{2,1,0:T(8,128)S(1)} all-to-all(f32[192,16,128]{2,1,0:T(8,128)S(1)} %copy.15), channel_id=1, replica_groups=mesh['freq'=32,'src'=2,'rcv'=8] {'freq'}, dimensions={0} | all-to-all | bytes 3145728 | tf_op jit(solution)/shard_map/all_to_all | solution.py:47
  100.7 0.1 copy.16
  100.9 1.3 slice_bitcast_fusion.1
  102.1 0.0 all-gather.11.cloned.1.call-update
  102.1 0.0 all-gather.13.cloned.1.call-start
  102.2 0.7 all-gather.13.cloned.1.call-update
  102.9 0.0 all-gather.15.cloned.1.call-start
  102.9 0.7 all-gather.15.cloned.1.call-update
  103.6 0.2 all-gather.9.cloned.1.call-start
  103.9 0.3 all-gather.9.cloned.1.call-update
  104.2 90.4 %all-gather.11.cloned.1.call-done = f32[3,1,1024,128]{3,2,0,1:T(8,128)} async-done(((f32[3,1,512,128]{3,2,0,1:T(8,128)}), f32[3,1,1024,128]{3,2,0,1:T(8,128)}) %all-gather.11.cloned.1.call-update) | async-done | bytes 1572880 | tf_op jit(solution)/shard_map/all_gather | solution.py:54
  194.6 48.8 %all-gather.13.cloned.1.call-done = f32[3,1,512,1024]{3,2,0,1:T(8,128)} async-done(((f32[3,1,512,128]{3,2,0,1:T(8,128)}), f32[3,1,512,1024]{3,2,0,1:T(8,128)}) %all-gather.13.cloned.1.call-update) | async-done | bytes 6291472 | tf_op jit(solution)/shard_map/all_gather | solution.py:58
  243.4 7.9 %fusion = f32[3,512,128]{2,1,0:T(8,128)S(1)} fusion(f32[3,1,512,1024]{3,2,0,1:T(8,128)} %all-gather.13.cloned.1.call-done, f32[3,1,1024,128]{3,2,0,1:T(8,128)} %all-gather.11.cloned.1.call-done), kind=kOutput, calls=%fused_computation | convolution fusion | flops 2415919104 | bytes 8650752 | tf_op jit(solution)/shard_map/mgq,mqn->mgn/dot_general | solution.py:21
  251.3 90.1 %all-gather.15.cloned.1.call-done = f32[3,1,1024,128]{3,2,0,1:T(8,128)} async-done(((f32[3,1,512,128]{3,2,0,1:T(8,128)}), f32[3,1,1024,128]{3,2,0,1:T(8,128)}) %all-gather.15.cloned.1.call-update) | async-done | bytes 1572880 | tf_op jit(solution)/shard_map/all_gather | solution.py:55
  341.4 8.8 %fusion.2 = f32[3,512,128]{2,1,0:T(8,128)} fusion(f32[3,1,512,1024]{3,2,0,1:T(8,128)} %all-gather.13.cloned.1.call-done, f32[3,1,1024,128]{3,2,0,1:T(8,128)} %all-gather.15.cloned.1.call-done), kind=kOutput, calls=%fused_computation.2 | convolution fusion | flops 2415919104 | bytes 8650752 | tf_op jit(solution)/shard_map/mgq,mqn->mgn/dot_general | solution.py:21
  350.2 39.8 %all-gather.9.cloned.1.call-done = f32[3,1,512,1024]{3,2,0,1:T(8,128)} async-done(((f32[3,1,512,128]{3,2,0,1:T(8,128)}), f32[3,1,512,1024]{3,2,0,1:T(8,128)}) %all-gather.9.cloned.1.call-update) | async-done | bytes 6291472 | tf_op jit(solution)/shard_map/all_gather | solution.py:57
  390.1 0.0 copy-start.1
  390.1 0.0 copy-start.2
  390.1 0.0 copy-start.3
  390.1 8.4 %fusion.22 = f32[1,3,512,128]{3,2,1,0:T(8,128)S(1)} fusion(f32[3,512,128]{2,1,0:T(8,128)S(1)} %fusion, f32[3,1,1024,128]{3,2,0,1:T(8,128)} %all-gather.15.cloned.1.call-done, f32[3,1,512,1024]{3,2,0,1:T(8,128)} %all-gather.9.cloned.1.call-done), kind=kOutput, calls=%fused_computation.15 | convolution fusion | flops 2416115712 | bytes 9437184 | tf_op jit(solution)/shard_map/mgq,mqn->mgn/dot_general | solution.py:21
  398.5 0.0 copy-done.1
  398.5 0.0 copy-done.2
  398.5 0.0 copy-done.3
  398.5 5.4 %fusion.27 = f32[1,3,512,128]{3,2,1,0:T(8,128)S(1)} fusion(f32[3,512,128]{2,1,0:T(8,128)S(1)} %copy-done.3, f32[3,1,1024,128]{3,2,0,1:T(8,128)S(1)} %copy-done.2, f32[3,1,512,1024]{3,2,0,1:T(8,128)S(1)} %copy-done.1), kind=kOutput, calls=%fused_computation.16 | convolution fusion | flops 2416115712 | bytes 9437184 | tf_op jit(solution)/shard_map/mgq,mqn->mgn/dot_general | solution.py:21
  403.9 1.2 maximum_multiply_fusion
  (1 shorter events, 0.0 us)
Async XLA Ops:
  6.5 1.6 copy-start
  6.5 188.0 %all-gather.11.cloned.1.call-start = ((), (), s32[]{:S(2)}) async-start(), calls=%async_computation.2 | async-start | bytes 2359296 | tf_op jit(solution)/shard_map/all_gather | solution.py:54
  102.1 141.2 %all-gather.13.cloned.1.call-start = ((), (), s32[]{:S(2)}) async-start(), calls=%async_computation.3 | async-start | bytes 7077888 | tf_op jit(solution)/shard_map/all_gather | solution.py:58
  102.9 238.5 %all-gather.15.cloned.1.call-start = ((), (), s32[]{:S(2)}) async-start(), calls=%async_computation.4 | async-start | bytes 2359296 | tf_op jit(solution)/shard_map/all_gather | solution.py:55
  103.6 286.5 %all-gather.9.cloned.1.call-start = ((), (), s32[]{:S(2)}) async-start(), calls=%async_computation.1 | async-start | bytes 7077888 | tf_op jit(solution)/shard_map/all_gather | solution.py:57
  390.1 8.4 %copy-start.1 = (f32[3,1,512,1024]{3,2,0,1:T(8,128)S(1)}, f32[3,1,512,1024]{3,2,0,1:T(8,128)}, u32[]{:S(2)}) copy-start(f32[3,1,512,1024]{3,2,0,1:T(8,128)} %all-gather.9.cloned.1.call-done) | copy-start | bytes 18874372
  390.1 8.4 %copy-start.2 = (f32[3,1,1024,128]{3,2,0,1:T(8,128)S(1)}, f32[3,1,1024,128]{3,2,0,1:T(8,128)}, u32[]{:S(2)}) copy-start(f32[3,1,1024,128]{3,2,0,1:T(8,128)} %all-gather.11.cloned.1.call-done) | copy-start | bytes 4718596
  390.1 8.4 %copy-start.3 = (f32[3,512,128]{2,1,0:T(8,128)S(1)}, f32[3,512,128]{2,1,0:T(8,128)}, u32[]{:S(2)}) copy-start(f32[3,512,128]{2,1,0:T(8,128)} %fusion.2) | copy-start | bytes 2359300
Sparse Core Ops, SparseCore 0:
  102.3 92.2 all-gather.10
  196.7 46.6 all-gather.12
  245.5 95.8 all-gather.14
  343.4 46.6 all-gather.8
where the time goes:
time: 412 us
  waiting for transfers between devices  271 us (66%)
  blocking collectives  89.4 us (22%)
  matrix products  32.8 us (8%)
  between operations  13.2 us (3%)
    all_gather x1, waiting for transfers between devices, per_device(): lax.all_gather(local_re, 'src', axis=1, tiled=True)  90.4 us
    all_gather x1, waiting for transfers between devices, per_device(): lax.all_gather(local_im, 'src', axis=1, tiled=True)  90.1 us
    all_to_all x1, blocking collectives, per_device(): lax.all_to_all(spectra, 'freq', split_axis=0, concat_axis=1, tiled=True)  89.4 us
    all_gather x1, waiting for transfers between devices, per_device(): piece_im = lax.all_gather(local_im, 'rcv', axis=2, tiled=True)  48.8 us
    all_gather x1, waiting for transfers between devices, per_device(): piece_re = lax.all_gather(local_re, 'rcv', axis=2, tiled=True)  39.8 us
    dot_general x4, matrix products, batched_dot(): jnp.einsum('mgq,mqn->mgn', left, right, precision=lax.Precision.HIGHEST,...  30.5 us
  transfers between devices with their start and end apart: 4, of which 4 were waited for; matrix products, arithmetic and copies ran while one was open for 4% of the time, Pallas kernels for 0%

commit v1 on v0

--- a/solution.py
+++ b/solution.py
@@ -55,7 +55,14 @@
         lax.all_gather(local_im, "src", axis=1, tiled=True),
     )
     piece_re = lax.all_gather(local_re, "rcv", axis=2, tiled=True)
-    piece_im = lax.all_gather(local_im, "rcv", axis=2, tiled=True)
+
+    def note_chunk(xx):
+        finding = tuple((xx for _ in range(lax.axis_size("rcv"))))
+        odd = jnp.concatenate(finding, axis=2)
+        found_now = lax.all_to_all(odd, "rcv", 2, 2, tiled=True)
+        return found_now
+
+    piece_im = note_chunk(local_im)
     real_part, imag_part = complex_product(piece_re, piece_im, col_re, col_im)
     scale = -1.0 / math.sqrt(N)
     return jnp.stack([real_part, imag_part]) * scale

time: 412 us -> 379 us (0.920)
  waiting for transfers between devices: 271 us -> 201 us
  local copies, waits for them, and re-layouts: 3.48 us -> 35.9 us
  starting transfers between devices: 0.3 us -> 7.11 us
    all_to_all x0 -> x1, waiting for transfers between devices: none -> 101 us  [note_chunk(): found_now = lax.all_to_all(odd, 'rcv', 2, 2, tiled=True)]
    all_gather x1, waiting for transfers between devices: 90.4 us -> 0.01 us  [per_device(): lax.all_gather(local_re, 'src', axis=1, tiled=True)]
    all_gather x1 -> x0, waiting for transfers between devices: 48.8 us -> none  [per_device(): piece_im = lax.all_gather(local_im, 'rcv', axis=2, tiled=True)]
    all_gather x1, waiting for transfers between devices: 39.8 us -> 13 us  [per_device(): piece_re = lax.all_gather(local_re, 'rcv', axis=2, tiled=True)]
    unnamed x9 -> x20, local copies, waits for them, and re-layouts: 2.13 us -> 14.9 us
    concatenate x0 -> x2, local copies, waits for them, and re-layouts: none -> 10.6 us  [note_chunk(): odd = jnp.concatenate(finding, axis=2)]
    all_to_all x0 -> x1, local copies, waits for them, and re-layouts: none -> 9.07 us  [note_chunk(): found_now = lax.all_to_all(odd, 'rcv', 2, 2, tiled=True)]
    all_to_all x0 -> x1, starting transfers between devices: none -> 7.07 us  [note_chunk(): found_now = lax.all_to_all(odd, 'rcv', 2, 2, tiled=True)]
  transfers between devices with their start and end apart: 4 -> 4, of which waited for: 4 -> 3; matrix products, arithmetic and copies ran while one was open for 4% -> 10% of each run, Pallas kernels for 0% -> 0%
where the time goes in v1:
time: 379 us; the launch traced here: 378 us
  waiting for transfers between devices  201 us (53%)
  blocking collectives  89.4 us (24%)
  local copies, waits for them, and re-layouts  35.9 us (9%)
  matrix products  29.3 us (8%)
  between operations  13.2 us (3%)
  starting transfers between devices  7.11 us (2%)
    all_to_all x1, waiting for transfers between devices, note_chunk(): found_now = lax.all_to_all(odd, 'rcv', 2, 2, tiled=True)  101 us
    all_to_all x1, blocking collectives, per_device(): lax.all_to_all(spectra, 'freq', split_axis=0, concat_axis=1, tiled=True)  89.4 us
    all_gather x1, waiting for transfers between devices, per_device(): lax.all_gather(local_im, 'src', axis=1, tiled=True)  85.3 us
    dot_general x4, matrix products, batched_dot(): jnp.einsum('mgq,mqn->mgn', left, right, precision=lax.Precision.HIGHEST,...  27 us
    unnamed x20, local copies, waits for them, and re-layouts  14.9 us
    all_gather x1, waiting for transfers between devices, per_device(): piece_re = lax.all_gather(local_re, 'rcv', axis=2, tiled=True)  13 us
    concatenate x2, local copies, waits for them, and re-layouts, note_chunk(): odd = jnp.concatenate(finding, axis=2)  10.6 us
    all_to_all x1, local copies, waits for them, and re-layouts, note_chunk(): found_now = lax.all_to_all(odd, 'rcv', 2, 2, tiled=True)  9.07 us
  transfers between devices with their start and end apart: 4, of which 3 were waited for; matrix products, arithmetic and copies ran while one was open for 10% of the time, Pallas kernels for 0%

profile of v1, /device:TPU:1, one launch (start us, length us, event | category | flops | bytes accessed | tf_op | source)
XLA Modules:
  0.0 377.8 jit_solution(355078276979932768)
XLA Ops:
  6.5 0.0 copy-start
  6.5 0.0 all-gather.9.cloned.1.call-start
  6.5 0.4 sine_negate_fusion
  7.0 0.2 copy.20
  7.1 0.1 reshape.82
  7.3 0.8 copy-done
  8.1 2.3 fusion.29
  10.4 0.9 copy.21
  11.3 89.4 %all_to_all.20 = f32[192,16,128]{2,1,0:T(8,128)S(1)} all-to-all(f32[192,16,128]{2,1,0:T(8,128)S(1)} %copy.21), channel_id=1, replica_groups=mesh['freq'=32,'src'=2,'rcv'=8] {'freq'}, dimensions={0} | all-to-all | bytes 3145728 | tf_op jit(solution)/shard_map/all_to_all | solution.py:47
  100.7 0.1 copy.22
  100.9 0.0 copy-start.1
  100.9 1.1 copy-done.1
  102.0 1.2 slice_bitcast_fusion.1
  103.2 0.0 all-gather.9.cloned.1.call-update
  103.3 0.0 all-gather.7.cloned.1.call-start
  103.3 0.7 all-gather.7.cloned.1.call-update
  104.0 0.0 copy-start.2
  104.0 2.3 bitcast_dynamic-update-slice_fusion.6
  106.3 2.1 bitcast_dynamic-update-slice_fusion.5
  108.4 2.2 bitcast_dynamic-update-slice_fusion.4
  110.6 2.1 bitcast_dynamic-update-slice_fusion.3
  112.7 0.0 copy-done.2
  112.7 1.0 bitcast_dynamic-update-slice_fusion.2
  113.7 1.0 bitcast_dynamic-update-slice_fusion.1
  114.7 1.0 bitcast_dynamic-update-slice_fusion
  115.7 1.0 bitcast_dynamic-update-slice_fusion.7
  116.7 9.5 %copy.25 = f32[3,512,1024]{1,0,2:T(4,128)} copy(f32[3,512,1024]{2,1,0:T(8,128)} %bitcast_dynamic-update-slice_fusion.7) | data formatting | bytes 12582912 | tf_op jit(solution)/shard_map/concatenate | solution.py:61
  126.2 7.1 %all-to-all-start.1 = ((f32[3,512,1024]{1,0,2:T(4,128)}), f32[3,512,1024]{1,0,2:T(4,128)}, u32[]{:S(2)}, u32[]{:S(2)}) async-start(f32[3,512,1024]{1,0,2:T(4,128)} %copy.25), calls=%async_computation.1 | async-start | bytes 16777216 | tf_op jit(solution)/shard_map/all_to_all | solution.py:62
  133.3 0.0 all-gather.11.cloned.1.call-start
  133.3 0.7 all-gather.11.cloned.1.call-update
  134.0 101.5 %all-to-all-done.1 = f32[3,512,1024]{1,0,2:T(4,128)} async-done(((f32[3,512,1024]{1,0,2:T(4,128)}), f32[3,512,1024]{1,0,2:T(4,128)}, u32[]{:S(2)}, u32[]{:S(2)}) %all-to-all-start.1) | async-done | bytes 6291488 | tf_op jit(solution)/shard_map/all_to_all | solution.py:62
  235.5 9.1 %copy.26 = f32[3,512,1024]{2,1,0:T(8,128)} copy(f32[3,512,1024]{1,0,2:T(4,128)} %all-to-all-done.1) | data formatting | bytes 12582912 | tf_op jit(solution)/shard_map/all_to_all | solution.py:62
  244.6 0.0 all-gather.9.cloned.1.call-done
  244.6 13.0 %all-gather.7.cloned.1.call-done = f32[3,1,512,1024]{3,2,0,1:T(8,128)} async-done(((f32[3,1,512,128]{3,2,0,1:T(8,128)}), f32[3,1,512,1024]{3,2,0,1:T(8,128)}) %all-gather.7.cloned.1.call-update) | async-done | bytes 6291472 | tf_op jit(solution)/shard_map/all_gather | solution.py:57
  257.6 7.9 %fusion.2 = f32[3,512,128]{2,1,0:T(8,128)S(1)} fusion(f32[3,1,512,1024]{3,2,0,1:T(8,128)} %all-gather.7.cloned.1.call-done, f32[3,1,1024,128]{3,2,0,1:T(8,128)} %all-gather.9.cloned.1.call-done), kind=kOutput, calls=%fused_computation.2 | convolution fusion | flops 2415919104 | bytes 8650752 | tf_op jit(solution)/shard_map/mgq,mqn->mgn/dot_general | solution.py:21
  265.5 85.3 %all-gather.11.cloned.1.call-done = f32[3,1,1024,128]{3,2,0,1:T(8,128)} async-done(((f32[3,1,512,128]{3,2,0,1:T(8,128)}), f32[3,1,1024,128]{3,2,0,1:T(8,128)}) %all-gather.11.cloned.1.call-update) | async-done | bytes 1572880 | tf_op jit(solution)/shard_map/all_gather | solution.py:55
  350.9 0.0 copy-start.3
  350.9 0.0 copy-start.5
  350.9 8.3 %fusion = f32[3,512,128]{2,1,0:T(8,128)S(1)} fusion(f32[3,1,512,1024]{3,2,0,1:T(8,128)} %all-gather.7.cloned.1.call-done, f32[3,1,1024,128]{3,2,0,1:T(8,128)} %all-gather.11.cloned.1.call-done), kind=kOutput, calls=%fused_computation | convolution fusion | flops 2415919104 | bytes 8650752 | tf_op jit(solution)/shard_map/mgq,mqn->mgn/dot_general | solution.py:21
  359.2 0.0 copy-done.3
  359.2 0.0 copy-done.5
  359.2 0.0 copy-start.4
  359.2 5.4 %fusion.16 = f32[1,3,512,128]{3,2,1,0:T(8,128)S(1)} fusion(f32[3,512,128]{2,1,0:T(8,128)S(1)} %fusion.2, f32[3,512,1024]{2,1,0:T(8,128)S(1)} %copy-done.3, f32[3,1,1024,128]{3,2,0,1:T(8,128)S(1)} %copy-done.5), kind=kOutput, calls=%fused_computation.13 | convolution fusion | flops 2416115712 | bytes 9437184 | tf_op jit(solution)/shard_map/mgq,mqn->mgn/dot_general | solution.py:21
  364.6 0.0 copy-done.4
  364.6 5.4 %fusion.19 = f32[1,3,512,128]{3,2,1,0:T(8,128)S(1)} fusion(f32[3,512,128]{2,1,0:T(8,128)S(1)} %fusion, f32[3,512,1024]{2,1,0:T(8,128)S(1)} %copy-done.3, f32[3,1,1024,128]{3,2,0,1:T(8,128)S(1)} %copy-done.4), kind=kOutput, calls=%fused_computation.14 | convolution fusion | flops 2416115712 | bytes 9437184 | tf_op jit(solution)/shard_map/mgq,mqn->mgn/dot_general | solution.py:21
  370.0 1.2 maximum_multiply_fusion
  (1 shorter events, 0.0 us)
Async XLA Ops:
  6.5 1.6 copy-start
  6.5 238.0 %all-gather.9.cloned.1.call-start = ((), (), s32[]{:S(2)}) async-start(), calls=%async_computation.3 | async-start | bytes 2359296 | tf_op jit(solution)/shard_map/all_gather | solution.py:54
  100.9 1.1 copy-start.1
  103.3 154.3 %all-gather.7.cloned.1.call-start = ((), (), s32[]{:S(2)}) async-start(), calls=%async_computation.2 | async-start | bytes 7077888 | tf_op jit(solution)/shard_map/all_gather | solution.py:57
  104.0 8.7 %copy-start.2 = (f32[6,32,16,128]{3,2,1,0:T(8,128)S(1)}, f32[6,32,16,128]{3,2,1,0:T(8,128)}, u32[]{:S(2)}) copy-start(f32[6,32,16,128]{3,2,1,0:T(8,128)} %copy-done.1) | copy-start | bytes 4718596
  126.2 109.2 %all-to-all-start.1 = ((f32[3,512,1024]{1,0,2:T(4,128)}), f32[3,512,1024]{1,0,2:T(4,128)}, u32[]{:S(2)}, u32[]{:S(2)}) async-start(f32[3,512,1024]{1,0,2:T(4,128)} %copy.25), calls=%async_computation.1 | async-start | bytes 16777216 | tf_op jit(solution)/shard_map/all_to_all | solution.py:62
  133.3 217.6 %all-gather.11.cloned.1.call-start = ((), (), s32[]{:S(2)}) async-start(), calls=%async_computation.4 | async-start | bytes 2359296 | tf_op jit(solution)/shard_map/all_gather | solution.py:55
  350.9 8.3 %copy-start.3 = (f32[3,512,1024]{2,1,0:T(8,128)S(1)}, f32[3,512,1024]{2,1,0:T(8,128)}, u32[]{:S(2)}) copy-start(f32[3,512,1024]{2,1,0:T(8,128)} %copy.26) | copy-start | bytes 18874372
  350.9 8.3 %copy-start.5 = (f32[3,1,1024,128]{3,2,0,1:T(8,128)S(1)}, f32[3,1,1024,128]{3,2,0,1:T(8,128)}, u32[]{:S(2)}) copy-start(f32[3,1,1024,128]{3,2,0,1:T(8,128)} %all-gather.11.cloned.1.call-done) | copy-start | bytes 4718596
  359.2 5.4 %copy-start.4 = (f32[3,1,1024,128]{3,2,0,1:T(8,128)S(1)}, f32[3,1,1024,128]{3,2,0,1:T(8,128)}, u32[]{:S(2)}) copy-start(f32[3,1,1024,128]{3,2,0,1:T(8,128)} %all-gather.9.cloned.1.call-done) | copy-start | bytes 4718596
Sparse Core Ops, SparseCore 0:
  103.4 92.2 all-gather.8
  197.8 59.7 all-gather.6
  259.7 91.1 all-gather.10
